TPU v7x, 256 devices: a whole 4x4x8 slice. The times are simulated.
256 devices in a mesh: leaf: 32 (over z, y), head: 8 (over x, core).
Axes of the slice: x: 4, y: 4, z: 8, core: 2. Of those that a mesh axis runs over, the one named last changes fastest.
Arguments:
- query_in: bfloat16 [4096, 8192], P('leaf', 'head'), may hold values from -12 to 12
- key_in: bfloat16 [4096, 1024], P(('leaf', 'head')), may hold values from -12 to 12
- value_in: bfloat16 [4096, 1024], P(('leaf', 'head')), may hold values from -6 to 6
- out_grad: bfloat16 [4096, 8192], P('leaf', 'head'), may hold values from -6 to 6
- ancestry: int32 [32, 8], replicated, may hold values from -1 to 31, as said below
- node_len: int32 [32], replicated, may hold values from 64 to 128, as said below
Outputs:
- attended: bfloat16 [4096, 8192], P('leaf', 'head')
- query_grad: float32 [4096, 8192], P('leaf', 'head')
- key_grad: float32 [4096, 1024], P(('leaf', 'head'))
- value_grad: float32 [4096, 1024], P(('leaf', 'head'))
Inputs may be any that keep to these rules, and one draw needn't show every extreme that they name: `ancestry`: row g lists the ancestors of node g from the root, node 0, at column 0 down to node g itself at column depth(g), then -1; every ancestor of a node comes before it; nodes 0 to 3 form a chain. `node_len`: the root's length is 128, the last node's 128 // 2.
All inputs are finite; a program needn't handle non-finite values.
Results may differ from a plain program's by a relative error of at most 0.019.
Values may be sent and summed in bfloat16 or wider, within the bound.
No kernel may reach another device: no remote copies, remote signals or barrier semaphores. Data moves between devices by JAX's collectives and lax.ppermute only.
A program may use at most 64 MiB of HBM per device.

v0:
```python
import math
import jax
import jax.numpy as jnp
from jax import lax
from jax.sharding import PartitionSpec as P

QH = 64
KVH = 8
HD = 128
BLK = 128
start_level = -1e30
tile_rows = 256


def over_tiles(length, update, carry):
    tile_width = math.gcd(length, tile_rows)
    return lax.fori_loop(
        0,
        length // tile_width,
        lambda number, state: update(state, number * tile_width, tile_width),
        carry,
    )


def token_tags(length_table, first, amount):
    position = first + jnp.arange(amount, dtype=jnp.int32)
    lengths = lax.dynamic_slice_in_dim(length_table, first, amount, 0)
    return (jnp.where(position % BLK < lengths, position // BLK, -2), position)


def visible(ancestor_rows, query_position, key_tag, key_position):
    member = jnp.any(ancestor_rows[:, :, None] == key_tag[None, None, :], axis=1)
    own_node = query_position // BLK
    return member & (
        (key_tag[None, :] != own_node[:, None]) | (key_position[None, :] <= query_position[:, None])
    )


def logits_of(query_group, key_tile, allowed):
    key_count = key_tile.shape[0]
    key_rows = key_tile.reshape(key_count, query_group.shape[1], HD)
    raw = jnp.einsum(
        "tkgd,skd->kgts", query_group, key_rows, preferred_element_type=jnp.float32
    ) * HD ** (-0.5)
    return jnp.where(allowed[None, None], raw, -jnp.inf)


def forward_tile(state, query_group, key_tile, value_tile, allowed):
    row_top, total, accum = state
    logits = logits_of(query_group, key_tile, allowed)
    new_top = jnp.maximum(row_top, jnp.max(logits, axis=-1))
    factor = jnp.exp(row_top - new_top)
    expo = jnp.exp(logits - new_top[..., None])
    total = total * factor + jnp.sum(expo, axis=-1)
    value_rows = value_tile.reshape(value_tile.shape[0], query_group.shape[1], HD)
    accum = accum * factor[..., None] + jnp.einsum(
        "kgts,skd->kgtd", expo.astype(jnp.bfloat16), value_rows, preferred_element_type=jnp.float32
    )
    return (new_top, total, accum)


def gradient_tile(query_group, grad_group, lse, delta, key_tile, value_tile, allowed):
    logits = logits_of(query_group, key_tile, allowed)
    weights = jnp.exp(logits - lse[..., None])
    value_rows = value_tile.reshape(value_tile.shape[0], query_group.shape[1], HD)
    dprob = jnp.einsum("tkgd,skd->kgts", grad_group, value_rows, preferred_element_type=jnp.float32)
    dlogit = (weights * (dprob - delta[..., None])).astype(jnp.bfloat16)
    return (weights.astype(jnp.bfloat16), dlogit)


def per_device(query_in, key_in, value_in, out_grad, ancestry, node_len):
    key_local, value_local = (
        lax.all_to_all(key_in, "head", split_axis=1, concat_axis=0, tiled=True),
        lax.all_to_all(value_in, "head", split_axis=1, concat_axis=0, tiled=True),
    )
    rows = query_in.shape[0]
    key_heads = key_local.shape[1] // HD
    group = QH // KVH
    leaf_base = lax.axis_index("leaf") * rows
    length_table = jnp.repeat(node_len, BLK)
    ancestor_table = jnp.repeat(ancestry, BLK, axis=0)
    all_rows = length_table.shape[0]
    query_position = leaf_base + jnp.arange(rows, dtype=jnp.int32)
    query_ancestors = lax.dynamic_slice_in_dim(ancestor_table, leaf_base, rows, 0)
    query_group = query_in.reshape(rows, key_heads, group, HD)
    grad_group = out_grad.reshape(rows, key_heads, group, HD)
    initial = (
        jnp.full((key_heads, group, rows), start_level, jnp.float32),
        jnp.zeros((key_heads, group, rows), jnp.float32),
        jnp.zeros((key_heads, group, rows, HD), jnp.float32),
    )
    key_piece = lax.all_gather(key_local, "leaf", axis=0, tiled=True)
    value_piece = lax.all_gather(value_local, "leaf", axis=0, tiled=True)

    def update(inner, offset, tile_width):
        key_tile = lax.dynamic_slice_in_dim(key_piece, offset, tile_width, 0)
        value_tile = lax.dynamic_slice_in_dim(value_piece, offset, tile_width, 0)
        key_tag, key_position = token_tags(length_table, offset, tile_width)
        allowed = visible(query_ancestors, query_position, key_tag, key_position)
        return forward_tile(inner, query_group, key_tile, value_tile, allowed)

    row_top, total, accum = over_tiles(key_piece.shape[0], update, initial)
    key_all, value_all = (
        lax.all_gather(key_local, "leaf", axis=0, tiled=True),
        lax.all_gather(value_local, "leaf", axis=0, tiled=True),
    )
    output = (accum / total[..., None]).astype(jnp.bfloat16)
    log_total = row_top + jnp.log(total)
    delta = jnp.sum(
        grad_group.transpose(1, 2, 0, 3).astype(jnp.float32) * output.astype(jnp.float32), axis=-1
    )
    attended = output.transpose(2, 0, 1, 3).reshape(rows, key_heads * group * HD)
    query_zero = jnp.zeros((rows, key_heads, group, HD), jnp.float32)

    def update_both(state, offset, tile_width):
        query_acc, buffer = state
        key_tile = lax.dynamic_slice_in_dim(key_all, offset, tile_width, 0)
        value_tile = lax.dynamic_slice_in_dim(value_all, offset, tile_width, 0)
        key_tag, key_position = token_tags(length_table, offset, tile_width)
        allowed = visible(query_ancestors, query_position, key_tag, key_position)
        probs, dlogit = gradient_tile(
            query_group, grad_group, log_total, delta, key_tile, value_tile, allowed
        )
        key_rows = key_tile.reshape(tile_width, key_heads, HD)
        query_acc = query_acc + jnp.einsum(
            "kgts,skd->tkgd", dlogit, key_rows, preferred_element_type=jnp.float32
        )
        key_term = jnp.einsum(
            "kgts,tkgd->skd", dlogit, query_group, preferred_element_type=jnp.float32
        )
        value_term = jnp.einsum(
            "kgts,tkgd->skd", probs, grad_group, preferred_element_type=jnp.float32
        )
        both_terms = jnp.concatenate(
            [
                key_term.reshape(tile_width, key_heads * HD),
                value_term.reshape(tile_width, key_heads * HD),
            ],
            axis=1,
        )
        buffer = lax.dynamic_update_slice_in_dim(buffer, both_terms, offset, 0)
        return (query_acc, buffer)

    buffer_zero = jnp.zeros((all_rows, 2 * key_heads * HD), jnp.float32)
    query_sum, buffer = over_tiles(all_rows, update_both, (query_zero, buffer_zero))
    summed = lax.psum_scatter(
        buffer.astype(jnp.bfloat16), "leaf", scatter_dimension=0, tiled=True
    ).astype(jnp.float32)
    key_sum = summed[:, : key_heads * HD]
    value_grad = summed[:, key_heads * HD :]
    scale = HD ** (-0.5)
    query_grad = (query_sum * scale).reshape(rows, key_heads * group * HD)
    key_grad = key_sum * scale
    key_grad, value_grad = (
        lax.all_to_all(
            key_grad.astype(jnp.bfloat16), "head", split_axis=0, concat_axis=1, tiled=True
        ).astype(key_grad.dtype),
        lax.all_to_all(
            value_grad.astype(jnp.bfloat16), "head", split_axis=0, concat_axis=1, tiled=True
        ).astype(value_grad.dtype),
    )
    return (attended, query_grad, key_grad, value_grad)


def solution(mesh):
    return jax.shard_map(
        per_device,
        mesh=mesh,
        in_specs=(
            P("leaf", "head"),
            P(("leaf", "head"), None),
            P(("leaf", "head"), None),
            P("leaf", "head"),
            P(),
            P(),
        ),
        out_specs=(
            P("leaf", "head"),
            P("leaf", "head"),
            P(("leaf", "head"), None),
            P(("leaf", "head"), None),
        ),
        check_vma=False,
    )
```

profile of v0, /device:TPU:1, one launch (start us, length us, event | category | flops | bytes accessed | tf_op | source)
XLA Modules:
  0.0 555.6 jit_solution(12811123765744551282)
XLA Ops:
  7.9 11.0 %all_to_all.64 = bf16[16,8,128]{2,0,1:T(8,128)(2,1)} all-to-all(bf16[16,8,128]{2,0,1:T(8,128)(2,1)S(1)} %copy_bitcast_fusion.3), channel_id=1, replica_groups=mesh['leaf'=32,'head'=8] {'head'}, dimensions={1} | all-to-all | bytes 65536 | tf_op jit(solution)/shard_map/all_to_all | solution.py:73
  19.7 8.5 %all_to_all.65 = bf16[16,8,128]{2,0,1:T(8,128)(2,1)} all-to-all(bf16[16,8,128]{2,0,1:T(8,128)(2,1)S(1)} %copy_bitcast_fusion.2), channel_id=1, replica_groups=mesh['leaf'=32,'head'=8] {'head'}, dimensions={1} | all-to-all | bytes 65536 | tf_op jit(solution)/shard_map/all_to_all | solution.py:74
  31.8 59.2 %all-gather.3.cloned.1.call-done = bf16[4096,128]{1,0:T(8,128)(2,1)} async-done(((bf16[128,128]{1,0:T(8,128)(2,1)}), bf16[4096,128]{1,0:T(8,128)(2,1)}) %all-gather.3.cloned.1.call-update) | async-done | bytes 1048592 | tf_op jit(solution)/shard_map/all_gather | solution.py:92
  91.0 76.5 %all-gather.5.cloned.1.call-done = bf16[4096,128]{1,0:T(8,128)(2,1)} async-done(((bf16[128,128]{1,0:T(8,128)(2,1)}), bf16[4096,128]{1,0:T(8,128)(2,1)}) %all-gather.5.cloned.1.call-update) | async-done | bytes 1048592 | tf_op jit(solution)/shard_map/all_gather | solution.py:93
  167.5 56.2 %while.44 = (s32[]{:T(128)}, f32[1,8,128]{2,1,0:T(8,128)S(1)}, f32[1,8,128]{2,1,0:T(8,128)S(1)}, f32[1,8,128,128]{3,2,1,0:T(8,128)S(1)}, s32[128,8]{1,0:T(8,128)...) while((s32[]{:T(128)}, f32[1,8,128]{2,1,0:T(8,128)S(1)}, ...), condition=%wide.region_4.5_spmd.clone.clone.clone, body=%wide.region_0.4_spmd.clone.clone.clone.sunk | while | flops 137082496 | bytes 4862171 | solution.py:17
  169.6 1.4 fusion.87
  173.1 1.4 fusion.87
  176.6 1.4 fusion.87
  180.1 1.4 fusion.87
  183.6 1.4 fusion.87
  187.1 1.4 fusion.87
  190.7 1.4 fusion.87
  194.2 1.4 fusion.87
  197.7 1.4 fusion.87
  201.2 1.4 fusion.87
  204.7 1.4 fusion.87
  208.2 1.4 fusion.87
  211.7 1.4 fusion.87
  215.2 1.4 fusion.87
  218.8 1.4 fusion.87
  222.3 1.4 fusion.87
  224.8 81.0 %while.45 = (s32[]{:T(128)}, f32[128,1,8,128]{0,3,2,1:T(8,128)S(1)}, bf16[4096,256]{1,0:T(8,128)(2,1)S(1)}, bf16[4096,128]{1,0:T(8,128)(2,1)}, s32[128,8]{1,0:T(...) while((s32[]{:T(128)}, ...), condition=%wide.region_8.9_spmd.clone.clone.clone, body=%wide.region_6.8_spmd.clone.clone.clone.sunk | while | flops 338534016 | bytes 8147185 | solution.py:17
  230.7 1.2 fusion.99
  235.7 1.2 fusion.99
  245.8 1.2 fusion.99
  305.8 1.3 copy-done.1
  307.2 216.1 %reduce-scatter.2.cloned.1.call-done = bf16[128,256]{1,0:T(8,128)(2,1)} async-done(((bf16[4096,256]{1,0:T(8,128)(2,1)}), bf16[128,256]{1,0:T(8,128)(2,1)}) %reduce-scatter.2.cloned.1.call-update) | async-done | bytes 65552 | tf_op jit(solution)/shard_map/reduce_scatter | solution.py:146
  523.3 1.5 multiply_convert_fusion
  524.8 10.3 %all-to-all-start.2 = ((bf16[8,16,128]{2,1,0:T(8,128)(2,1)}), bf16[8,16,128]{2,1,0:T(8,128)(2,1)S(1)}, u32[]{:S(2)}, u32[]{:S(2)}) async-start(bf16[8,16,128]{2,1,0:T(8,128)(2,1)} %bitcast.14), calls=%async_computation.3 | async-start | bytes 65536 | tf_op jit(solution)/shard_map/all_to_all | solution.py:155
  537.6 2.2 all-to-all-done.2
  539.8 4.0 all-to-all-start.3
  544.4 4.1 all-to-all-done.3
  (403 shorter events, 118.6 us)
Async XLA Ops:
  7.2 0.8 copy-start
  7.2 24.5 %copy-start.4 = (s32[32]{0:T(128)S(1)}, s32[32]{0:T(128)}, u32[]{:S(2)}) copy-start(s32[32]{0:T(128)} %param.15) | copy-start | bytes 388
  7.2 83.8 %all-gather.3.cloned.1.call-start = ((), (), s32[]{:S(2)}) async-start(), calls=%async_computation.5 | async-start | bytes 1081344 | tf_op jit(solution)/shard_map/all_gather | solution.py:92
  18.9 148.6 %all-gather.5.cloned.1.call-start = ((), (), s32[]{:S(2)}) async-start(), calls=%async_computation.6 | async-start | bytes 1081344 | tf_op jit(solution)/shard_map/all_gather | solution.py:93
  28.2 495.1 %reduce-scatter.2.cloned.1.call-start = ((), (), s32[]{:S(2)}) async-start(), calls=%async_computation.7 | async-start | bytes 2162688 | tf_op jit(solution)/shard_map/reduce_scatter | solution.py:146
  305.8 1.3 copy-start.1
  305.8 229.3 %copy-start.2 = (bf16[1,8,128,128]{2,3,1,0:T(8,128)(2,1)S(1)}, bf16[1,8,128,128]{2,3,1,0:T(8,128)(2,1)}, u32[]{:S(2)}) copy-start(bf16[1,8,128,128]{2,3,1,0:T(8,128)(2,1)} %get-tuple-element.949) | copy-start | bytes 786436
  523.3 13.6 %copy-start.3 = (bf16[128,256]{1,0:T(8,128)(2,1)S(1)}, bf16[128,256]{1,0:T(8,128)(2,1)}, u32[]{:S(2)}) copy-start(bf16[128,256]{1,0:T(8,128)(2,1)} %reduce-scatter.2.cloned.1.call-done) | copy-start | bytes 196612
  524.8 15.0 %all-to-all-start.2 = ((bf16[8,16,128]{2,1,0:T(8,128)(2,1)}), bf16[8,16,128]{2,1,0:T(8,128)(2,1)S(1)}, u32[]{:S(2)}, u32[]{:S(2)}) async-start(bf16[8,16,128]{2,1,0:T(8,128)(2,1)} %bitcast.14), calls=%async_computation.3 | async-start | bytes 65536 | tf_op jit(solution)/shard_map/all_to_all | solution.py:155
  539.8 8.7 %all-to-all-start.3 = ((bf16[8,16,128]{2,1,0:T(8,128)(2,1)}), bf16[8,16,128]{2,1,0:T(8,128)(2,1)S(1)}, u32[]{:S(2)}, u32[]{:S(2)}) async-start(bf16[8,16,128]{2,1,0:T(8,128)(2,1)} %bitcast.16), calls=%async_computation.4 | async-start | bytes 65536 | tf_op jit(solution)/shard_map/all_to_all | solution.py:158
Sparse Core Ops, SparseCore 0:
  19.0 71.9 all-gather.2
  93.6 73.8 all-gather.4
  307.3 215.9 reduce-scatter.1
where the time goes:
time: 560 us; the launch traced here: 556 us
  waiting for transfers between devices  358 us (64%)
  matrix products  106 us (19%)
  other arithmetic  25.9 us (5%)
  blocking collectives  19.4 us (3%)
  local copies, waits for them, and re-layouts  14.7 us (3%)
  starting transfers between devices  14.4 us (3%)
  between operations  13.9 us (2%)
    reduce_scatter x1, waiting for transfers between devices, per_device(): lax.psum_scatter(buffer.astype(jnp.bfloat16), 'leaf', scatter_dimension=0...  216 us
    all_gather x1, waiting for transfers between devices, per_device(): value_piece = lax.all_gather(value_local, 'leaf', axis=0, tiled=True)  76.5 us
    all_gather x1, waiting for transfers between devices, per_device(): key_piece = lax.all_gather(key_local, 'leaf', axis=0, tiled=True)  59.2 us
    dot_general x32, matrix products, logits_of(): jnp.einsum('tkgd,skd->kgts', query_group, key_rows, preferred_element_typ...  37.6 us
    dot_general x16, matrix products, forward_tile(): jnp.einsum('kgts,skd->kgtd', expo.astype(jnp.bfloat16), value_rows, prefe...  21.8 us
    dot_general x16, matrix products, update_both(): jnp.einsum('kgts,skd->tkgd', dlogit, key_rows, preferred_element_type=jnp...  18.5 us
    dot_general x16, matrix products, gradient_tile(): jnp.einsum('tkgd,skd->kgts', grad_group, value_rows, preferred_element_ty...  18.1 us
    reduce_or x32, other arithmetic, visible(): jnp.any(ancestor_rows[:, :, None] == key_tag[None, None, :], axis=1)  13 us
  transfers between devices with their start and end apart: 5, of which 5 were waited for; matrix products, arithmetic and copies ran while one was open for 1% of the time, Pallas kernels for 0%

commit v1 on v0

--- a/solution.py
+++ b/solution.py
@@ -89,8 +89,13 @@
         jnp.zeros((key_heads, group, rows), jnp.float32),
         jnp.zeros((key_heads, group, rows, HD), jnp.float32),
     )
-    key_piece = lax.all_gather(key_local, "leaf", axis=0, tiled=True)
-    value_piece = lax.all_gather(value_local, "leaf", axis=0, tiled=True)
+    key_piece, value_piece = jnp.split(
+        lax.all_gather(
+            jnp.concatenate([key_local, value_local], axis=1), "leaf", axis=0, tiled=True
+        ),
+        [key_local.shape[1]],
+        axis=1,
+    )
 
     def update(inner, offset, tile_width):
         key_tile = lax.dynamic_slice_in_dim(key_piece, offset, tile_width, 0)

time: 560 us -> 590 us (1.054)
  waiting for transfers between devices: 358 us -> 404 us
  matrix products: 106 us -> 92.5 us
  blocking collectives: 19.4 us -> 7.8 us
  starting transfers between devices: 14.4 us -> 20.8 us
    all_gather x2 -> x3, waiting for transfers between devices: 136 us -> 177 us  [the longest x1 77.1 us: per_device(): lax.all_gather(value_local, 'leaf', axis=0, tiled=True)]
    dot_general x16, matrix products: 21.8 us -> 8.42 us  [forward_tile(): jnp.einsum('kgts,skd->kgtd', expo.astype(jnp.bfloat16), value_rows, prefe...]
    all_to_all x1 -> x0, blocking collectives: 11 us -> none  [per_device(): lax.all_to_all(key_in, 'head', split_axis=1, concat_axis=0, tiled=True)]
    all_to_all x0 -> x1, starting transfers between devices: none -> 6.44 us  [per_device(): lax.all_to_all(key_in, 'head', split_axis=1, concat_axis=0, tiled=True)]
  transfers between devices with their start and end apart: 5 -> 7, of which waited for: 5 -> 7; matrix products, arithmetic and copies ran while one was open for 1% -> 9% of each run, Pallas kernels for 0% -> 0%
where the time goes in v1:
time: 590 us; the launch traced here: 587 us
  waiting for transfers between devices  404 us (68%)
  matrix products  92.5 us (16%)
  other arithmetic  26.6 us (5%)
  starting transfers between devices  20.8 us (4%)
  local copies, waits for them, and re-layouts  18.1 us (3%)
  between operations  13.9 us (2%)
  blocking collectives  7.8 us (1%)
    reduce_scatter x1, waiting for transfers between devices, per_device(): lax.psum_scatter(buffer.astype(jnp.bfloat16), 'leaf', scatter_dimension=0...  216 us
    all_gather x1, waiting for transfers between devices, per_device(): lax.all_gather(value_local, 'leaf', axis=0, tiled=True)  77.1 us
    all_gather x1, waiting for transfers between devices, per_device(): lax.all_gather(jnp.concatenate([key_local, value_local], axis=1), 'leaf',...  69.6 us
    dot_general x32, matrix products, logits_of(): jnp.einsum('tkgd,skd->kgts', query_group, key_rows, preferred_element_typ...  37.6 us
    all_gather x1, waiting for transfers between devices, per_device(): lax.all_gather(key_local, 'leaf', axis=0, tiled=True)  29.9 us
    dot_general x16, matrix products, update_both(): jnp.einsum('kgts,skd->tkgd', dlogit, key_rows, preferred_element_type=jnp...  18.5 us
    dot_general x16, matrix products, gradient_tile(): jnp.einsum('tkgd,skd->kgts', grad_group, value_rows, preferred_element_ty...  18.1 us
    reduce_or x32, other arithmetic, visible(): jnp.any(ancestor_rows[:, :, None] == key_tag[None, None, :], axis=1)  13 us
  transfers between devices with their start and end apart: 7, of which 7 were waited for; matrix products, arithmetic and copies ran while one was open for 9% of the time, Pallas kernels for 0%

profile of v1, /device:TPU:1, one launch (start us, length us, event | category | flops | bytes accessed | tf_op | source)
XLA Modules:
  0.0 586.6 jit_solution(18204764403016852198)
XLA Ops:
  8.5 6.4 %all-to-all-start = ((bf16[16,8,128]{2,0,1:T(8,128)(2,1)}), bf16[16,8,128]{2,0,1:T(8,128)(2,1)S(1)}, u32[]{:S(2)}, u32[]{:S(2)}) async-start(bf16[16,8,128]{2,0,1:T(8,128)(2,1)} %copy_bitcast_fusion.3), calls=%async_computation | async-start | bytes 65536 | tf_op jit(solution)/shard_map/all_to_all | solution.py:73
  15.8 4.0 all-to-all-done
  19.7 7.8 %all_to_all.64 = bf16[16,8,128]{2,0,1:T(8,128)(2,1)S(1)} all-to-all(bf16[16,8,128]{2,0,1:T(8,128)(2,1)S(1)} %copy_bitcast_fusion.2), channel_id=1, replica_groups=mesh['leaf'=32,'head'=8] {'head'}, dimensions={1} | all-to-all | bytes 65536 | tf_op jit(solution)/shard_map/all_to_all | solution.py:74
  32.6 69.6 %all-gather.4.cloned.1.call-done = bf16[4096,256]{1,0:T(8,128)(2,1)} async-done(((bf16[128,256]{1,0:T(8,128)(2,1)}), bf16[4096,256]{1,0:T(8,128)(2,1)}) %all-gather.4.cloned.1.call-update) | async-done | bytes 2097168 | tf_op jit(solution)/shard_map/all_gather | solution.py:93
  102.2 2.7 fusion.56
  104.9 42.8 %while.44 = (s32[]{:T(128)}, f32[1,8,128]{2,1,0:T(8,128)S(1)}, f32[1,8,128]{2,1,0:T(8,128)S(1)}, f32[1,8,128,128]{3,2,1,0:T(8,128)S(1)}, s32[128,8]{1,0:T(8,128)...) while((s32[]{:T(128)}, f32[1,8,128]{2,1,0:T(8,128)S(1)}, ...), condition=%wide.region_4.5_spmd.clone.clone.clone, body=%wide.region_0.4_spmd.clone.clone.clone.sunk | while | flops 137082496 | bytes 4862171 | solution.py:17
  148.7 29.9 %all-gather.6.cloned.1.call-done = bf16[4096,128]{1,0:T(8,128)(2,1)} async-done(((bf16[128,128]{1,0:T(8,128)(2,1)}), bf16[4096,128]{1,0:T(8,128)(2,1)}) %all-gather.6.cloned.1.call-update) | async-done | bytes 1048592 | tf_op jit(solution)/shard_map/all_gather | solution.py:109
  178.6 77.1 %all-gather.8.cloned.1.call-done = bf16[4096,128]{1,0:T(8,128)(2,1)} async-done(((bf16[128,128]{1,0:T(8,128)(2,1)}), bf16[4096,128]{1,0:T(8,128)(2,1)}) %all-gather.8.cloned.1.call-update) | async-done | bytes 1048592 | tf_op jit(solution)/shard_map/all_gather | solution.py:110
  255.8 81.0 %while.45 = (s32[]{:T(128)}, f32[128,1,8,128]{0,3,2,1:T(8,128)S(1)}, bf16[4096,256]{1,0:T(8,128)(2,1)S(1)}, bf16[4096,128]{1,0:T(8,128)(2,1)}, s32[128,8]{1,0:T(...) while((s32[]{:T(128)}, ...), condition=%wide.region_8.9_spmd.clone.clone.clone, body=%wide.region_6.8_spmd.clone.clone.clone.sunk | while | flops 338534016 | bytes 8147185 | solution.py:17
  256.6 1.2 fusion.100
  261.7 1.2 fusion.100
  266.7 1.2 fusion.100
  271.8 1.2 fusion.100
  276.9 1.2 fusion.100
  281.9 1.2 fusion.100
  287.0 1.2 fusion.100
  292.0 1.2 fusion.100
  297.1 1.2 fusion.100
  302.2 1.2 fusion.100
  307.2 1.2 fusion.100
  312.3 1.2 fusion.100
  317.3 1.2 fusion.100
  322.4 1.2 fusion.100
  327.5 1.2 fusion.100
  332.5 1.2 fusion.100
  336.8 1.3 copy-done.1
  338.2 216.1 %reduce-scatter.2.cloned.1.call-done = bf16[128,256]{1,0:T(8,128)(2,1)} async-done(((bf16[4096,256]{1,0:T(8,128)(2,1)}), bf16[128,256]{1,0:T(8,128)(2,1)}) %reduce-scatter.2.cloned.1.call-update) | async-done | bytes 65552 | tf_op jit(solution)/shard_map/reduce_scatter | solution.py:151
  554.3 1.5 multiply_convert_fusion
  555.8 10.2 %all-to-all-start.2 = ((bf16[8,16,128]{2,1,0:T(8,128)(2,1)}), bf16[8,16,128]{2,1,0:T(8,128)(2,1)S(1)}, u32[]{:S(2)}, u32[]{:S(2)}) async-start(bf16[8,16,128]{2,1,0:T(8,128)(2,1)} %bitcast.16), calls=%async_computation.3 | async-start | bytes 65536 | tf_op jit(solution)/shard_map/all_to_all | solution.py:160
  568.5 2.2 all-to-all-done.2
  570.7 4.0 all-to-all-start.3
  575.4 4.1 all-to-all-done.3
  (413 shorter events, 113.6 us)
Async XLA Ops:
  7.2 0.8 copy-start
  8.5 11.2 %all-to-all-start = ((bf16[16,8,128]{2,0,1:T(8,128)(2,1)}), bf16[16,8,128]{2,0,1:T(8,128)(2,1)S(1)}, u32[]{:S(2)}, u32[]{:S(2)}) async-start(bf16[16,8,128]{2,0,1:T(8,128)(2,1)} %copy_bitcast_fusion.3), calls=%async_computation | async-start | bytes 65536 | tf_op jit(solution)/shard_map/all_to_all | solution.py:73
  15.0 87.2 %all-gather.4.cloned.1.call-start = ((), (), s32[]{:S(2)}) async-start(), calls=%async_computation.5 | async-start | bytes 2162688 | tf_op jit(solution)/shard_map/all_gather | solution.py:93
  15.8 16.7 %copy-start.6 = (s32[32]{0:T(128)S(1)}, s32[32]{0:T(128)}, u32[]{:S(2)}) copy-start(s32[32]{0:T(128)} %param.15) | copy-start | bytes 388
  19.7 8.5 %copy-start.3 = (bf16[16,8,128]{2,0,1:T(8,128)(2,1)}, bf16[16,8,128]{2,0,1:T(8,128)(2,1)S(1)}, u32[]{:S(2)}) copy-start(bf16[16,8,128]{2,0,1:T(8,128)(2,1)S(1)} %all-to-all-done) | copy-start | bytes 98308
  27.5 5.0 copy-start.4
  28.2 150.4 %all-gather.6.cloned.1.call-start = ((), (), s32[]{:S(2)}) async-start(), calls=%async_computation.6 | async-start | bytes 1081344 | tf_op jit(solution)/shard_map/all_gather | solution.py:109
  29.0 226.7 %all-gather.8.cloned.1.call-start = ((), (), s32[]{:S(2)}) async-start(), calls=%async_computation.7 | async-start | bytes 1081344 | tf_op jit(solution)/shard_map/all_gather | solution.py:110
  32.5 521.8 %reduce-scatter.2.cloned.1.call-start = ((), (), s32[]{:S(2)}) async-start(), calls=%async_computation.8 | async-start | bytes 2162688 | tf_op jit(solution)/shard_map/reduce_scatter | solution.py:151
  336.8 1.3 copy-start.1
  336.8 229.2 %copy-start.2 = (bf16[1,8,128,128]{2,3,1,0:T(8,128)(2,1)S(1)}, bf16[1,8,128,128]{2,3,1,0:T(8,128)(2,1)}, u32[]{:S(2)}) copy-start(bf16[1,8,128,128]{2,3,1,0:T(8,128)(2,1)} %get-tuple-element.949) | copy-start | bytes 786436
  554.3 13.6 %copy-start.5 = (bf16[128,256]{1,0:T(8,128)(2,1)S(1)}, bf16[128,256]{1,0:T(8,128)(2,1)}, u32[]{:S(2)}) copy-start(bf16[128,256]{1,0:T(8,128)(2,1)} %reduce-scatter.2.cloned.1.call-done) | copy-start | bytes 196612
  555.8 15.0 %all-to-all-start.2 = ((bf16[8,16,128]{2,1,0:T(8,128)(2,1)}), bf16[8,16,128]{2,1,0:T(8,128)(2,1)S(1)}, u32[]{:S(2)}, u32[]{:S(2)}) async-start(bf16[8,16,128]{2,1,0:T(8,128)(2,1)} %bitcast.16), calls=%async_computation.3 | async-start | bytes 65536 | tf_op jit(solution)/shard_map/all_to_all | solution.py:160
  570.7 8.7 %all-to-all-start.3 = ((bf16[8,16,128]{2,1,0:T(8,128)(2,1)}), bf16[8,16,128]{2,1,0:T(8,128)(2,1)S(1)}, u32[]{:S(2)}, u32[]{:S(2)}) async-start(bf16[8,16,128]{2,1,0:T(8,128)(2,1)} %bitcast.18), calls=%async_computation.4 | async-start | bytes 65536 | tf_op jit(solution)/shard_map/all_to_all | solution.py:163
Sparse Core Ops, SparseCore 0:
  28.3 73.8 all-gather.3
  105.4 73.2 all-gather.5
  181.8 73.8 all-gather.7
  338.3 215.9 reduce-scatter.1
